TPU v7x, 256 devices: a whole 4x4x8 slice. The times are simulated.
256 devices in a mesh: pair: 32 (over x, z_hi, y), rows: 8 (over z_lo, core).
Axes of the slice: x: 4, y: 4, z: 8 (z_hi: 2, z_lo: 4; z = z_hi * 4 + z_lo), core: 2. Of those that a mesh axis runs over, the one named last changes fastest.
Arguments:
- samples: float32 [32768, 4096], P(('pair', 'rows')), may hold values from -400 to 400
- keep_mask: int32 [256, 8], P(('pair', 'rows')), may hold values 0 or 1
- keep_rate: float32 [8], replicated, may hold values from 0.5 to 1
Outputs:
- cosine: float32 [64, 512, 512], P('pair', 'rows')
All inputs are finite; a program needn't handle non-finite values. No bound on the sum of `keep_mask` on one device may be relied on, other than what follows from the above.
Results may differ from a plain program's by a relative error of at most 0.00005.
Values sent between devices are 32-bit elements; how exact they have to be, the bound alone decides.
A program may use at most 128 MiB of HBM per device.

v0:
```python
import jax
import jax.numpy as jnp
from jax import lax
from jax.sharding import Mesh
from jax.sharding import PartitionSpec as P

BLOCKS = 8
BLOCK_COLS = 512
BLOCK_ROWS = 128
COLS = 4096
PAIR = ("pair_0", "pair_1", "pair_2")
ROWS = ("rows_0", "rows_1")
PAIR_ROWS = ("pair_0", "pair_1", "pair_2", "rows_0", "rows_1")
EPS = 1e-06


def one_axis_at_a_time(value, axes):
    for axis in axes:
        value = lax.psum(value, axis)
    return value


def reduced_to_own(tiles, axes, turns):
    inside = tiles.shape[1:]
    tiles = tiles.reshape(*(lax.axis_size(a) for a in axes), *inside)
    tiles = jnp.moveaxis(tiles, turns, range(len(axes))).reshape(-1, *inside)
    for k in turns:
        tiles = lax.psum_scatter(tiles, axes[k], scatter_dimension=0, tiled=True)
    return tiles[0]


def in_blocks(value, dim, count):
    lengths = value.shape
    tiles = value.reshape(*lengths[:dim], count, lengths[dim] // count, *lengths[dim + 1 :])
    return jnp.moveaxis(tiles, dim, 0)


def scatter_axes(value, axes, turns, dim):
    count = lax.axis_size(axes)
    return reduced_to_own(in_blocks(value, dim, count), axes, turns)


def per_device(samples, keep_mask, keep_rate):
    pair_count = lax.axis_size(PAIR)
    row_count = lax.axis_size(ROWS)
    tile_count = BLOCKS * BLOCKS // pair_count
    pair_index = lax.axis_index(PAIR)
    row_index = lax.axis_index(ROWS)
    local_rows = samples.shape[0]
    slice_rows = BLOCK_COLS // row_count
    squares = jnp.sum(samples * samples, axis=0)
    col_norms = jnp.sqrt(one_axis_at_a_time(squares, PAIR_ROWS) + EPS)
    weights = keep_mask.astype(jnp.float32)
    masked = (
        samples.reshape(local_rows // BLOCK_ROWS, BLOCK_ROWS, BLOCKS, BLOCK_COLS)
        * weights[:, None, :, None]
    )
    masked_rows = masked.reshape(local_rows, COLS)
    initial = jnp.zeros((BLOCKS * BLOCKS, slice_rows, BLOCK_COLS), jnp.float32)
    piece = lax.all_gather(masked_rows, ROWS, axis=0, tiled=True)
    count = piece.shape[0]
    split_cols = piece.reshape(count, BLOCKS, row_count, slice_rows)
    left_cols = lax.dynamic_slice_in_dim(split_cols, row_index, 1, 2)[:, :, 0, :]
    right_cols = piece.reshape(count, BLOCKS, BLOCK_COLS)
    product = jnp.einsum(
        "rai,rbj->abij",
        left_cols,
        right_cols,
        precision=lax.Precision.HIGHEST,
        preferred_element_type=jnp.float32,
    )
    tile_grams = product.reshape(initial.shape)
    summed = scatter_axes(tile_grams, PAIR, (0, 2, 1), 0)
    first_tile = pair_index * tile_count
    left_block = first_tile // BLOCKS
    right_start = first_tile % BLOCKS
    norm_blocks = col_norms.reshape(BLOCKS, BLOCK_COLS)
    row_norms = lax.dynamic_slice(
        norm_blocks, (left_block, row_index * slice_rows), (1, slice_rows)
    )[0]
    col_part = lax.dynamic_slice(norm_blocks, (right_start, jnp.int32(0)), (tile_count, BLOCK_COLS))
    left_rate = lax.dynamic_slice(keep_rate, (left_block,), (1,))
    right_rate = lax.dynamic_slice(keep_rate, (right_start,), (tile_count,))
    row_scale = left_rate * row_norms
    col_scale = right_rate[:, None] * col_part
    return summed / (row_scale[None, :, None] * col_scale[:, None, :])


def solution(mesh):
    finer = Mesh(
        mesh.devices.reshape(4, 2, 4, 4, 2), ("pair_0", "pair_1", "pair_2", "rows_0", "rows_1")
    )
    placed = (P(PAIR_ROWS, None), P(PAIR_ROWS, None), P())
    return jax.shard_map(
        per_device, mesh=finer, in_specs=placed, out_specs=P(PAIR, ROWS, None), check_vma=False
    )
```

profile of v0, /device:TPU:1, one launch (start us, length us, event | category | flops | bytes accessed | tf_op | source)
XLA Modules:
  0.0 418.9 jit_solution(9704003310913359644)
XLA Ops:
  6.5 0.0 copy-start.1
  6.5 0.0 all-gather.2.cloned.1.call-start
  6.5 1.9 copy.6
  8.5 0.0 copy-done.1
  8.5 0.1 broadcast_bitcast_fusion
  8.6 2.0 broadcast_multiply_fusion
  10.5 0.0 all-gather.2.cloned.1.call-update
  10.6 0.0 reduce-scatter.4.cloned.1.call-start
  10.6 175.9 %all-gather.2.cloned.1.call-done = f32[1024,4096]{0,1:T(8,128)} async-done(((f32[128,4096]{0,1:T(8,128)}), f32[1024,4096]{0,1:T(8,128)}) %all-gather.2.cloned.1.call-update) | async-done | bytes 16777232 | tf_op jit(solution)/shard_map/all_gather | solution.py:60
  186.5 30.1 %fusion = f32[8,512,8,64]{1,3,2,0:T(8,128)S(1)} fusion(f32[1024,8,512,1]{0,2,3,1:T(8,128)} %bitcast.30, f32[1024,8,8,64]{0,3,2,1:T(8,128)} %bitcast.31, s32[]{:T(128)S(6)} %select_n.25), kind=kOutput, calls=%fused_computation | convolution fusion | flops 25769803776 | bytes 27262980 | tf_op jit(solution)/shard_map/rai,rbj->abij/dot_general | solution.py:65
  216.6 4.3 %copy.8 = f32[4,4,2,2,64,512]{5,4,3,2,1,0:T(8,128)} copy(f32[4,4,2,2,64,512]{5,4,2,0,3,1:T(8,128)S(1)} %bitcast.28) | data formatting | bytes 16777216 | tf_op jit(solution)/shard_map/transpose | solution.py:26
  220.9 0.0 reduce-scatter.4.cloned.1.call-update
  220.9 0.0 copy-start
  221.0 0.0 reduce-scatter.6.cloned.1.call-start
  221.0 82.4 %reduce-scatter.4.cloned.1.call-done = f32[8,2,64,512]{3,2,1,0:T(8,128)} async-done(((f32[32,2,64,512]{3,2,1,0:T(8,128)}), f32[8,2,64,512]{3,2,1,0:T(8,128)}) %reduce-scatter.4.cloned.1.call-update) | async-done | bytes 2097168 | tf_op jit(solution)/shard_map/reduce_scatter | solution.py:28
  303.4 0.0 reduce-scatter.6.cloned.1.call-update
  303.5 0.0 reduce-scatter.8.cloned.1.call-start
  303.5 34.6 %reduce-scatter.6.cloned.1.call-done = f32[2,2,64,512]{3,2,1,0:T(8,128)} async-done(((f32[8,2,64,512]{3,2,1,0:T(8,128)}), f32[2,2,64,512]{3,2,1,0:T(8,128)}) %reduce-scatter.6.cloned.1.call-update) | async-done | bytes 524304 | tf_op jit(solution)/shard_map/reduce_scatter | solution.py:28
  338.1 0.0 reduce-scatter.8.cloned.1.call-update
  338.2 0.0 copy-done
  338.2 0.2 multiply_reduce_fusion
  338.3 13.1 %psum.35 = f32[4096]{0:T(1024)S(1)} all-reduce(f32[4096]{0:T(1024)S(1)} %multiply_reduce_fusion), channel_id=1, replica_groups=mesh['pair_0'=4,'pair_1'=2,'pair_2'=4,'rows_0'=4,'rows_1'=2] {'pair_0'}, use_global_device_ids=true, to_apply=%region_4.0 | all-reduce | flops 4096 | bytes 32768 | tf_op jit(solution)/shard_map/psum | solution.py:19
  351.4 18.0 %psum.36 = f32[4096]{0:T(1024)S(1)} all-reduce(f32[4096]{0:T(1024)S(1)} %psum.35), channel_id=1, replica_groups=mesh['pair_0'=4,'pair_1'=2,'pair_2'=4,'rows_0'=4,'rows_1'=2] {'pair_1'}, use_global_device_ids=true, to_apply=%region_5.0 | all-reduce | flops 4096 | bytes 32768 | tf_op jit(solution)/shard_map/psum | solution.py:19
  369.4 12.0 %psum.37 = f32[4096]{0:T(1024)S(1)} all-reduce(f32[4096]{0:T(1024)S(1)} %psum.36), channel_id=1, replica_groups=mesh['pair_0'=4,'pair_1'=2,'pair_2'=4,'rows_0'=4,'rows_1'=2] {'pair_2'}, use_global_device_ids=true, to_apply=%region_6.0 | all-reduce | flops 4096 | bytes 32768 | tf_op jit(solution)/shard_map/psum | solution.py:19
  381.4 12.4 %psum.38 = f32[4096]{0:T(1024)S(1)} all-reduce(f32[4096]{0:T(1024)S(1)} %psum.37), channel_id=1, replica_groups=mesh['pair_0'=4,'pair_1'=2,'pair_2'=4,'rows_0'=4,'rows_1'=2] {'rows_0'}, use_global_device_ids=true, to_apply=%region_7.0 | all-reduce | flops 4096 | bytes 32768 | tf_op jit(solution)/shard_map/psum | solution.py:19
  393.8 15.3 %psum.39 = f32[4096]{0:T(1024)S(1)} all-reduce(f32[4096]{0:T(1024)S(1)} %psum.38), channel_id=1, replica_groups=mesh['pair_0'=4,'pair_1'=2,'pair_2'=4,'rows_0'=4,'rows_1'=2] {'rows_1'}, use_global_device_ids=true, to_apply=%region_8.0 | all-reduce | flops 4096 | bytes 32768 | tf_op jit(solution)/shard_map/psum | solution.py:19
  409.2 0.0 copy-done.2
  409.2 0.1 dynamic_slice.18
  409.3 0.6 dynamic_slice.16
  409.8 0.7 multiply_bitcast_fusion
  410.6 0.1 dynamic-slice_multiply_fusion
  410.6 1.8 bitcast_divide_fusion
  (6 shorter events, 0.0 us)
Async XLA Ops:
  6.5 1.9 copy-start.1
  6.5 180.0 %all-gather.2.cloned.1.call-start = ((), (), s32[]{:S(2)}) async-start(), calls=%async_computation.3 | async-start | bytes 18874368 | tf_op jit(solution)/shard_map/all_gather | solution.py:60
  10.6 292.9 %reduce-scatter.4.cloned.1.call-start = ((), (), s32[]{:S(2)}) async-start(), calls=%async_computation.4 | async-start | bytes 10485760 | tf_op jit(solution)/shard_map/reduce_scatter | solution.py:28
  220.9 117.2 %copy-start = (f32[128,4096]{1,0:T(8,128)S(1)}, f32[128,4096]{1,0:T(8,128)}, u32[]{:S(2)}) copy-start(f32[128,4096]{1,0:T(8,128)} %param.3) | copy-start | bytes 6291460
  221.0 117.1 %reduce-scatter.6.cloned.1.call-start = ((), (), s32[]{:S(2)}) async-start(), calls=%async_computation.5 | async-start | bytes 2621440 | tf_op jit(solution)/shard_map/reduce_scatter | solution.py:28
  303.4 105.7 %copy-start.2 = (f32[8]{0:T(128)S(1)}, f32[8]{0:T(128)}, u32[]{:S(2)}) copy-start(f32[8]{0:T(128)} %param.5) | copy-start | bytes 100
  303.5 107.2 %reduce-scatter.8.cloned.1.call-start = ((), (), s32[]{:S(2)}) async-start(), calls=%async_computation.6 | async-start | bytes 786432 | tf_op jit(solution)/shard_map/reduce_scatter | solution.py:28
Sparse Core Ops, SparseCore 0:
  10.7 175.8 all-gather.1
  221.1 82.3 reduce-scatter.3
  306.0 32.0 reduce-scatter.5
  340.4 29.7 reduce-scatter.7
where the time goes:
time: 419 us
  waiting for transfers between devices  293 us (70%)
  blocking collectives  70.8 us (17%)
  matrix products  30.1 us (7%)
  between operations  13.2 us (3%)
  local copies, waits for them, and re-layouts  6.96 us (2%)
  other arithmetic  4.7 us (1%)
    all_gather x1, waiting for transfers between devices, per_device(): piece = lax.all_gather(masked_rows, ROWS, axis=0, tiled=True)  176 us
    reduce_scatter x3, waiting for transfers between devices, reduced_to_own(): tiles = lax.psum_scatter(tiles, axes[k], scatter_dimension=0, tiled=True)  117 us
    psum x5, blocking collectives, one_axis_at_a_time(): value = lax.psum(value, axis)  70.8 us
    dot_general x1, matrix products, per_device(): jnp.einsum('rai,rbj->abij', left_cols, right_cols, precision=lax.Precisio...  30.1 us
  transfers between devices with their start and end apart: 4, of which 3 were waited for; matrix products, arithmetic and copies ran while one was open for 0% of the time, Pallas kernels for 0%

commit v1 on v0

--- a/solution.py
+++ b/solution.py
@@ -57,7 +57,10 @@
     )
     masked_rows = masked.reshape(local_rows, COLS)
     initial = jnp.zeros((BLOCKS * BLOCKS, slice_rows, BLOCK_COLS), jnp.float32)
-    piece = lax.all_gather(masked_rows, ROWS, axis=0, tiled=True)
+    size = lax.axis_size(ROWS)
+    blocks = jnp.stack([masked_rows for _ in range(size)])
+    blocks = lax.all_to_all(blocks, ROWS, split_axis=0, concat_axis=0)
+    piece = jnp.concatenate(blocks, axis=0)
     count = piece.shape[0]
     split_cols = piece.reshape(count, BLOCKS, row_count, slice_rows)
     left_cols = lax.dynamic_slice_in_dim(split_cols, row_index, 1, 2)[:, :, 0, :]

time: 419 us -> 704 us (1.68)
  waiting for transfers between devices: 293 us -> 482 us
  local copies, waits for them, and re-layouts: 6.96 us -> 87.9 us
  starting transfers between devices: 0.12 us -> 8.91 us
    all_to_all x0 -> x1, waiting for transfers between devices: none -> 363 us  [per_device(): blocks = lax.all_to_all(blocks, ROWS, split_axis=0, concat_axis=0)]
    all_gather x1 -> x0, waiting for transfers between devices: 176 us -> none  [per_device(): piece = lax.all_gather(masked_rows, ROWS, axis=0, tiled=True)]
    all_to_all x0 -> x2, local copies, waits for them, and re-layouts: none -> 35.2 us  [per_device(): blocks = lax.all_to_all(blocks, ROWS, split_axis=0, concat_axis=0)]
    another operation x0 -> x2, local copies, waits for them, and re-layouts: none -> 24.8 us  [the longest x1 18 us: per_device(): split_cols = piece.reshape(count, BLOCKS, row_count, slice_rows)]
    unnamed x9 -> x5, local copies, waits for them, and re-layouts: 2.01 us -> 21.1 us
    all_to_all x0 -> x1, starting transfers between devices: none -> 8.83 us  [per_device(): blocks = lax.all_to_all(blocks, ROWS, split_axis=0, concat_axis=0)]
where the time goes in v1:
time: 704 us; the launch traced here: 703 us
  waiting for transfers between devices  482 us (68%)
  local copies, waits for them, and re-layouts  87.9 us (12%)
  blocking collectives  70.6 us (10%)
  matrix products  33.9 us (5%)
  between operations  13.2 us (2%)
  starting transfers between devices  8.91 us (1%)
    all_to_all x1, waiting for transfers between devices, per_device(): blocks = lax.all_to_all(blocks, ROWS, split_axis=0, concat_axis=0)  363 us
    reduce_scatter x3, waiting for transfers between devices, reduced_to_own(): tiles = lax.psum_scatter(tiles, axes[k], scatter_dimension=0, tiled=True)  119 us
    psum x5, blocking collectives, one_axis_at_a_time(): value = lax.psum(value, axis)  70.6 us
    all_to_all x2, local copies, waits for them, and re-layouts, per_device(): blocks = lax.all_to_all(blocks, ROWS, split_axis=0, concat_axis=0)  35.2 us
    dot_general x1, matrix products, per_device(): jnp.einsum('rai,rbj->abij', left_cols, right_cols, precision=lax.Precisio...  33.9 us
    unnamed x5, local copies, waits for them, and re-layouts  21.1 us
    another operation x1, local copies, waits for them, and re-layouts, per_device(): split_cols = piece.reshape(count, BLOCKS, row_count, slice_rows)  18 us
  transfers between devices with their start and end apart: 4, of which 3 were waited for; matrix products, arithmetic and copies ran while one was open for 0% of the time, Pallas kernels for 0%

profile of v1, /device:TPU:1, one launch (start us, length us, event | category | flops | bytes accessed | tf_op | source)
XLA Modules:
  0.0 703.0 jit_solution(9471174515130418064)
XLA Ops:
  6.5 0.7 convert_bitcast_fusion
  7.2 0.1 broadcast_bitcast_fusion
  7.3 3.2 multiply_reduce_fusion
  10.5 1.9 copy.9
  12.4 6.8 stack.3
  19.2 8.8 %all-to-all-start = ((f32[8,128,4096]{1,2,0:T(8,128)}), f32[8,128,4096]{1,2,0:T(8,128)}, u32[]{:S(2)}, u32[]{:S(2)}) async-start(f32[8,128,4096]{1,2,0:T(8,128)} %stack.3), calls=%async_computation | async-start | bytes 33554432 | tf_op jit(solution)/shard_map/all_to_all | solution.py:62
  28.0 0.0 reduce-scatter.4.cloned.1.call-start
  28.0 362.8 %all-to-all-done = f32[8,128,4096]{1,2,0:T(8,128)} async-done(((f32[8,128,4096]{1,2,0:T(8,128)}), f32[8,128,4096]{1,2,0:T(8,128)}, u32[]{:S(2)}, u32[]{:S(2)}) %all-to-all-start) | async-done | bytes 16777248 | tf_op jit(solution)/shard_map/all_to_all | solution.py:62
  390.8 17.5 %copy.10 = f32[8,128,4096]{2,1,0:T(8,128)} copy(f32[8,128,4096]{1,2,0:T(8,128)} %all-to-all-done) | data formatting | bytes 33554432 | tf_op jit(solution)/shard_map/all_to_all | solution.py:62
  408.3 21.0 %copy.18 = f32[128,8,8,512]{3,2,1,0:T(8,128)} copy(f32[128,8,8,512]{3,1,2,0:T(8,128)} %bitcast.27) | data formatting | bytes 33554432
  429.3 17.7 %copy.11 = f32[8,128,4096]{1,0,2:T(8,128)} copy(f32[8,128,4096]{1,2,0:T(8,128)} %all-to-all-done) | data formatting | bytes 33554432 | tf_op jit(solution)/shard_map/all_to_all | solution.py:62
  447.0 18.0 %reshape_reshape.7 = f32[1024,8,8,64]{0,3,2,1:T(8,128)} reshape(f32[8,128,4096]{1,0,2:T(8,128)} %copy.11) | data formatting | bytes 33554432 | tf_op jit(solution)/shard_map/reshape;reshape | solution.py:65
  465.0 33.9 %fusion = f32[8,512,8,64]{1,3,2,0:T(8,128)S(1)} fusion(f32[1024,8,512,1]{2,1,0,3:T(8,128)} %bitcast.29, f32[1024,8,8,64]{0,3,2,1:T(8,128)} %reshape_reshape.7, s32[]{:T(128)S(6)} %select_n.25), kind=kOutput, calls=%fused_computation | convolution fusion | flops 25769803776 | bytes 27262980 | tf_op jit(solution)/shard_map/rai,rbj->abij/dot_general | solution.py:68
  498.9 4.3 copy.13
  503.2 0.0 reduce-scatter.4.cloned.1.call-update
  503.2 0.0 reduce-scatter.6.cloned.1.call-start
  503.2 84.7 %reduce-scatter.4.cloned.1.call-done = f32[8,2,64,512]{3,2,1,0:T(8,128)} async-done(((f32[32,2,64,512]{3,2,1,0:T(8,128)}), f32[8,2,64,512]{3,2,1,0:T(8,128)}) %reduce-scatter.4.cloned.1.call-update) | async-done | bytes 2097168 | tf_op jit(solution)/shard_map/reduce_scatter | solution.py:28
  587.9 0.0 reduce-scatter.6.cloned.1.call-update
  587.9 0.0 reduce-scatter.8.cloned.1.call-start
  588.0 34.5 %reduce-scatter.6.cloned.1.call-done = f32[2,2,64,512]{3,2,1,0:T(8,128)} async-done(((f32[8,2,64,512]{3,2,1,0:T(8,128)}), f32[2,2,64,512]{3,2,1,0:T(8,128)}) %reduce-scatter.6.cloned.1.call-update) | async-done | bytes 524304 | tf_op jit(solution)/shard_map/reduce_scatter | solution.py:28
  622.5 0.0 reduce-scatter.8.cloned.1.call-update
  622.6 0.0 copy-done
  622.6 0.6 dynamic_slice.16
  623.2 0.1 dynamic_slice.18
  623.3 13.0 %psum.35 = f32[4096]{0:T(1024)S(1)} all-reduce(f32[4096]{0:T(1024)S(1)} %get-tuple-element.5), channel_id=1, replica_groups=mesh['pair_0'=4,'pair_1'=2,'pair_2'=4,'rows_0'=4,'rows_1'=2] {'pair_0'}, use_global_device_ids=true, to_apply=%region_4.0 | all-reduce | flops 4096 | bytes 32768 | tf_op jit(solution)/shard_map/psum | solution.py:19
  636.3 17.6 %psum.36 = f32[4096]{0:T(1024)S(1)} all-reduce(f32[4096]{0:T(1024)S(1)} %psum.35), channel_id=1, replica_groups=mesh['pair_0'=4,'pair_1'=2,'pair_2'=4,'rows_0'=4,'rows_1'=2] {'pair_1'}, use_global_device_ids=true, to_apply=%region_5.0 | all-reduce | flops 4096 | bytes 32768 | tf_op jit(solution)/shard_map/psum | solution.py:19
  653.9 13.3 %psum.37 = f32[4096]{0:T(1024)S(1)} all-reduce(f32[4096]{0:T(1024)S(1)} %psum.36), channel_id=1, replica_groups=mesh['pair_0'=4,'pair_1'=2,'pair_2'=4,'rows_0'=4,'rows_1'=2] {'pair_2'}, use_global_device_ids=true, to_apply=%region_6.0 | all-reduce | flops 4096 | bytes 32768 | tf_op jit(solution)/shard_map/psum | solution.py:19
  667.2 12.0 %psum.38 = f32[4096]{0:T(1024)S(1)} all-reduce(f32[4096]{0:T(1024)S(1)} %psum.37), channel_id=1, replica_groups=mesh['pair_0'=4,'pair_1'=2,'pair_2'=4,'rows_0'=4,'rows_1'=2] {'rows_0'}, use_global_device_ids=true, to_apply=%region_7.0 | all-reduce | flops 4096 | bytes 32768 | tf_op jit(solution)/shard_map/psum | solution.py:19
  679.2 14.6 %psum.39 = f32[4096]{0:T(1024)S(1)} all-reduce(f32[4096]{0:T(1024)S(1)} %psum.38), channel_id=1, replica_groups=mesh['pair_0'=4,'pair_1'=2,'pair_2'=4,'rows_0'=4,'rows_1'=2] {'rows_1'}, use_global_device_ids=true, to_apply=%region_8.0 | all-reduce | flops 4096 | bytes 32768 | tf_op jit(solution)/shard_map/psum | solution.py:19
  693.9 0.7 multiply_bitcast_fusion
  694.6 0.1 dynamic-slice_multiply_fusion
  694.7 1.8 bitcast_divide_fusion
  (5 shorter events, 0.0 us)
Async XLA Ops:
  19.2 371.6 %all-to-all-start = ((f32[8,128,4096]{1,2,0:T(8,128)}), f32[8,128,4096]{1,2,0:T(8,128)}, u32[]{:S(2)}, u32[]{:S(2)}) async-start(f32[8,128,4096]{1,2,0:T(8,128)} %stack.3), calls=%async_computation | async-start | bytes 33554432 | tf_op jit(solution)/shard_map/all_to_all | solution.py:62
  28.0 559.9 %reduce-scatter.4.cloned.1.call-start = ((), (), s32[]{:S(2)}) async-start(), calls=%async_computation.4 | async-start | bytes 10485760 | tf_op jit(solution)/shard_map/reduce_scatter | solution.py:28
  503.2 119.4 %copy-start = (f32[8]{0:T(128)S(1)}, f32[8]{0:T(128)}, u32[]{:S(2)}) copy-start(f32[8]{0:T(128)} %param.5) | copy-start | bytes 100
  503.2 119.3 %reduce-scatter.6.cloned.1.call-start = ((), (), s32[]{:S(2)}) async-start(), calls=%async_computation.5 | async-start | bytes 2621440 | tf_op jit(solution)/shard_map/reduce_scatter | solution.py:28
  587.9 106.7 %reduce-scatter.8.cloned.1.call-start = ((), (), s32[]{:S(2)}) async-start(), calls=%async_computation.6 | async-start | bytes 786432 | tf_op jit(solution)/shard_map/reduce_scatter | solution.py:28
Sparse Core Ops, SparseCore 0:
  503.3 84.5 reduce-scatter.3
  590.4 32.0 reduce-scatter.5
  625.0 29.7 reduce-scatter.7

commit v2 on v0

--- a/solution.py
+++ b/solution.py
@@ -16,7 +16,12 @@
 
 def one_axis_at_a_time(value, axes):
     for axis in axes:
-        value = lax.psum(value, axis)
+
+        def trace_wires_on_mesh(body):
+            parts_out = jnp.sum(lax.all_gather(body, axis_name=axis), axis=0)
+            return parts_out
+
+        value = trace_wires_on_mesh(value)
     return value
 
 

time: 419 us -> 399 us (0.952)
  blocking collectives: 70.8 us -> 50.2 us
    psum x5 -> x0, blocking collectives: 70.8 us -> none  [one_axis_at_a_time(): value = lax.psum(value, axis)]
    all_gather x0 -> x5, blocking collectives: none -> 50.2 us  [trace_wires_on_mesh(): parts_out = jnp.sum(lax.all_gather(body, axis_name=axis), axis=0)]
where the time goes in v2:
time: 399 us
  waiting for transfers between devices  293 us (73%)
  blocking collectives  50.2 us (13%)
  matrix products  30.1 us (8%)
  between operations  13.3 us (3%)
  local copies, waits for them, and re-layouts  7.08 us (2%)
  other arithmetic  4.9 us (1%)
    all_gather x1, waiting for transfers between devices, per_device(): piece = lax.all_gather(masked_rows, ROWS, axis=0, tiled=True)  176 us
    reduce_scatter x3, waiting for transfers between devices, reduced_to_own(): tiles = lax.psum_scatter(tiles, axes[k], scatter_dimension=0, tiled=True)  117 us
    all_gather x5, blocking collectives, trace_wires_on_mesh(): parts_out = jnp.sum(lax.all_gather(body, axis_name=axis), axis=0)  50.2 us
    dot_general x1, matrix products, per_device(): jnp.einsum('rai,rbj->abij', left_cols, right_cols, precision=lax.Precisio...  30.1 us
  transfers between devices with their start and end apart: 4, of which 3 were waited for; matrix products, arithmetic and copies ran while one was open for 0% of the time, Pallas kernels for 0%

profile of v2, /device:TPU:1, one launch (start us, length us, event | category | flops | bytes accessed | tf_op | source)
XLA Modules:
  0.0 398.8 jit_solution(9222064761971149449)
XLA Ops:
  6.5 0.0 all-gather.7.cloned.1.call-start
  6.5 1.9 copy.12
  8.5 0.0 copy-done.1
  8.5 0.1 broadcast_bitcast_fusion
  8.6 2.0 broadcast_multiply_fusion
  10.5 0.0 all-gather.7.cloned.1.call-update
  10.6 0.0 reduce-scatter.4.cloned.1.call-start
  10.6 175.9 %all-gather.7.cloned.1.call-done = f32[1024,4096]{0,1:T(8,128)} async-done(((f32[128,4096]{0,1:T(8,128)}), f32[1024,4096]{0,1:T(8,128)}) %all-gather.7.cloned.1.call-update) | async-done | bytes 16777232 | tf_op jit(solution)/shard_map/all_gather | solution.py:65
  186.5 30.1 %fusion = f32[8,512,8,64]{1,3,2,0:T(8,128)S(1)} fusion(f32[1024,8,512,1]{0,2,3,1:T(8,128)} %bitcast.30, f32[1024,8,8,64]{0,3,2,1:T(8,128)} %bitcast.31, s32[]{:T(128)S(6)} %select_n.25), kind=kOutput, calls=%fused_computation | convolution fusion | flops 25769803776 | bytes 27262980 | tf_op jit(solution)/shard_map/rai,rbj->abij/dot_general | solution.py:70
  216.6 4.3 %copy.14 = f32[4,4,2,2,64,512]{5,4,3,2,1,0:T(8,128)} copy(f32[4,4,2,2,64,512]{5,4,2,0,3,1:T(8,128)S(1)} %bitcast.28) | data formatting | bytes 16777216 | tf_op jit(solution)/shard_map/transpose | solution.py:31
  220.9 0.0 reduce-scatter.4.cloned.1.call-update
  220.9 0.0 copy-start
  221.0 0.0 reduce-scatter.6.cloned.1.call-start
  221.0 82.4 %reduce-scatter.4.cloned.1.call-done = f32[8,2,64,512]{3,2,1,0:T(8,128)} async-done(((f32[32,2,64,512]{3,2,1,0:T(8,128)}), f32[8,2,64,512]{3,2,1,0:T(8,128)}) %reduce-scatter.4.cloned.1.call-update) | async-done | bytes 2097168 | tf_op jit(solution)/shard_map/reduce_scatter | solution.py:33
  303.4 0.0 reduce-scatter.6.cloned.1.call-update
  303.5 0.0 copy-start.2
  303.5 0.0 reduce-scatter.8.cloned.1.call-start
  303.5 34.6 %reduce-scatter.6.cloned.1.call-done = f32[2,2,64,512]{3,2,1,0:T(8,128)} async-done(((f32[8,2,64,512]{3,2,1,0:T(8,128)}), f32[2,2,64,512]{3,2,1,0:T(8,128)}) %reduce-scatter.6.cloned.1.call-update) | async-done | bytes 524304 | tf_op jit(solution)/shard_map/reduce_scatter | solution.py:33
  338.1 0.0 reduce-scatter.8.cloned.1.call-update
  338.2 0.0 copy-done
  338.2 0.2 multiply_reduce_fusion
  338.3 9.3 %all-gather = f32[16384]{0:T(1024)S(1)} all-gather(f32[4096]{0:T(1024)S(1)} %multiply_reduce_fusion), channel_id=2, replica_groups=mesh['pair_0'=4,'pair_1'=2,'pair_2'=4,'rows_0'=4,'rows_1'=2] {'pair_0'}, dimensions={0}, use_global_device_ids=true | all-gather | bytes 81920 | tf_op jit(solution)/shard_map/all_gather | solution.py:21
  347.7 7.3 %all-gather.1 = f32[8192]{0:T(1024)S(1)} all-gather(f32[4096]{0:T(1024)S(1)} %reduce_sum.55), channel_id=3, replica_groups=mesh['pair_0'=4,'pair_1'=2,'pair_2'=4,'rows_0'=4,'rows_1'=2] {'pair_1'}, dimensions={0}, use_global_device_ids=true | all-gather | bytes 49152 | tf_op jit(solution)/shard_map/all_gather | solution.py:21
  355.0 10.2 %all-gather.2 = f32[16384]{0:T(1024)S(1)} all-gather(f32[4096]{0:T(1024)S(1)} %reduce_sum.56), channel_id=4, replica_groups=mesh['pair_0'=4,'pair_1'=2,'pair_2'=4,'rows_0'=4,'rows_1'=2] {'pair_2'}, dimensions={0}, use_global_device_ids=true | all-gather | bytes 81920 | tf_op jit(solution)/shard_map/all_gather | solution.py:21
  365.3 10.6 %all-gather.3 = f32[16384]{0:T(1024)S(1)} all-gather(f32[4096]{0:T(1024)S(1)} %reduce_sum.57), channel_id=5, replica_groups=mesh['pair_0'=4,'pair_1'=2,'pair_2'=4,'rows_0'=4,'rows_1'=2] {'rows_0'}, dimensions={0}, use_global_device_ids=true | all-gather | bytes 81920 | tf_op jit(solution)/shard_map/all_gather | solution.py:21
  376.0 12.9 %all-gather.4 = f32[8192]{0:T(1024)S(1)} all-gather(f32[4096]{0:T(1024)S(1)} %reduce_sum.58), channel_id=6, replica_groups=mesh['pair_0'=4,'pair_1'=2,'pair_2'=4,'rows_0'=4,'rows_1'=2] {'rows_1'}, dimensions={0}, use_global_device_ids=true | all-gather | bytes 49152 | tf_op jit(solution)/shard_map/all_gather | solution.py:21
  389.0 0.0 copy-done.2
  389.0 0.1 dynamic_slice.18
  389.1 0.6 dynamic_slice.16
  389.7 0.7 multiply_bitcast_fusion
  390.4 0.1 dynamic-slice_multiply_fusion
  390.5 1.8 bitcast_divide_fusion
  (16 shorter events, 0.4 us)
Async XLA Ops:
  6.5 1.9 copy-start.1
  6.5 180.0 %all-gather.7.cloned.1.call-start = ((), (), s32[]{:S(2)}) async-start(), calls=%async_computation.3 | async-start | bytes 18874368 | tf_op jit(solution)/shard_map/all_gather | solution.py:65
  10.6 292.9 %reduce-scatter.4.cloned.1.call-start = ((), (), s32[]{:S(2)}) async-start(), calls=%async_computation.4 | async-start | bytes 10485760 | tf_op jit(solution)/shard_map/reduce_scatter | solution.py:33
  220.9 117.2 %copy-start = (f32[128,4096]{1,0:T(8,128)S(1)}, f32[128,4096]{1,0:T(8,128)}, u32[]{:S(2)}) copy-start(f32[128,4096]{1,0:T(8,128)} %param.3) | copy-start | bytes 6291460
  221.0 117.1 %reduce-scatter.6.cloned.1.call-start = ((), (), s32[]{:S(2)}) async-start(), calls=%async_computation.5 | async-start | bytes 2621440 | tf_op jit(solution)/shard_map/reduce_scatter | solution.py:33
  303.5 85.5 %copy-start.2 = (f32[8]{0:T(128)S(1)}, f32[8]{0:T(128)}, u32[]{:S(2)}) copy-start(f32[8]{0:T(128)} %param.5) | copy-start | bytes 100
  303.5 87.0 %reduce-scatter.8.cloned.1.call-start = ((), (), s32[]{:S(2)}) async-start(), calls=%async_computation.6 | async-start | bytes 786432 | tf_op jit(solution)/shard_map/reduce_scatter | solution.py:33
Sparse Core Ops, SparseCore 0:
  10.7 175.8 all-gather.6
  221.1 82.3 reduce-scatter.3
  306.0 32.0 reduce-scatter.5
  340.4 25.8 reduce-scatter.7
